TPU v7x, 512 devices: a whole 4x8x8 slice. The times are simulated.
512 devices in a mesh: seq: 64 (over z, x, core), head: 8 (over y).
Axes of the slice: x: 4, y: 8, z: 8, core: 2. Of those that a mesh axis runs over, the one named last changes fastest.
Arguments:
- xbc: bfloat16 [24576, 10240], P('seq', 'head'), may hold values from -6 to 6
- gate_z: bfloat16 [24576, 8192], P('seq', 'head'), may hold values from -6 to 6
- dt_raw: bfloat16 [128, 24576], P('head', 'seq'), may hold values from -3 to 3
- dt_bias: float32 [128], P('head'), may hold values from -1 to 0.5
- a_log: float32 [128], P('head'), may hold values from -11.5 to -6.6
- skip_d: float32 [128], P('head'), may hold values from 0.5 to 1.5
- conv_weight: float32 [4, 10240], P(None, 'head'), may hold values from -3 to 3
- conv_bias: float32 [10240], P('head'), may hold values from -3 to 3
- norm_gain: float32 [8192], P('head'), may hold values from 0.1 to 1.9
- out_weight: bfloat16 [8192, 4096], P('head', 'seq'), may hold values from -0.1875 to 0.1875
- starts: int32 [24576], P('seq'), may hold values from 0 to 1, as said below
Outputs:
- mixed: bfloat16 [24576, 4096], P('seq', 'head')
Inputs may be any that keep to these rules, and one draw needn't show every extreme that they name: `starts`: a 0 or 1 flag for every token; every 1 lies among the first 6144 tokens, and there is at least one.
All inputs are finite; a program needn't handle non-finite values.
Results may differ from a plain program's by a relative error of at most 0.013.
Values may be sent and summed in bfloat16 or wider, within the bound.
A program may use at most 128 MiB of HBM per device.

v0:
```python
import jax
import jax.numpy as jnp
from jax import lax
from jax.sharding import PartitionSpec as P

P_SIZE = 64
N = 128
DI = 8192
HG = 16
GW = 1280


def carried_in(part, axis, combine, identity):
    place = lax.axis_index(axis)
    gathered = jax.tree.map(lambda a: lax.all_gather(a, axis), part)
    state = jax.tree.map(lambda a, e: jnp.zeros_like(a) + jnp.asarray(e, a.dtype), part, identity)

    def one(hop, state):
        return combine(
            state, jax.tree.map(lambda a: lax.dynamic_index_in_dim(a, hop, 0, False), gathered)
        )

    return lax.fori_loop(0, place, one, state)


def passed_along(block, axis, distance):
    devices = range(lax.axis_size(axis))
    route = [(i - distance, i) for i in devices if i - distance in devices]
    return lax.ppermute(block, axis, route)


def combine(earlier, later):
    return (earlier[0] * later[0], later[0][:, None, None] * earlier[1] + later[1])


def chain_states(decays, states):
    identity = (jnp.ones_like(decays), jnp.zeros_like(states))
    result = carried_in((decays, states), "seq", combine, identity)
    return result[1]


def block_local(item):
    xc, bc, cc, dtc, lc, sc = item
    cumul = jnp.cumsum(lc, axis=1)
    runs = jnp.cumsum(sc)
    tail = (
        jnp.where(
            (runs == runs[-1])[None, :], jnp.exp(jnp.minimum(cumul[:, -1:] - cumul, 0.0)), 0.0
        )
        * dtc
    )
    b_heads = jnp.repeat(bc, HG, axis=1)
    scaled = (tail[:, :, None] * jnp.swapaxes(b_heads, 0, 1).astype(jnp.float32)).astype(
        jnp.bfloat16
    )
    local = jnp.einsum("shp,hsn->hpn", xc, scaled, preferred_element_type=jnp.float32)
    total = jnp.exp(cumul[:, -1]) * (runs[-1] == 0).astype(jnp.float32)
    enter = jnp.exp(cumul) * (runs == 0).astype(jnp.float32)[None, :]
    return (local, total, enter)


def block_inner(item):
    xc, bc, cc, dtc, lc, sc = item
    length = xc.shape[0]
    cumul = jnp.cumsum(lc, axis=1)
    runs = jnp.cumsum(sc)
    lower = jnp.arange(length)[:, None] >= jnp.arange(length)[None, :]
    same = lower & (runs[:, None] == runs[None, :])
    diff = cumul[:, :, None] - cumul[:, None, :]
    wdec = jnp.where(same[None], jnp.exp(jnp.minimum(diff, 0.0)), 0.0)
    scores = jnp.einsum("tgn,sgn->gts", cc, bc, preferred_element_type=jnp.float32)
    scores_h = jnp.repeat(scores, HG, axis=0)
    weights = (scores_h * wdec * dtc[:, None, :]).astype(jnp.bfloat16)
    return jnp.einsum("hts,shp->thp", weights, xc, preferred_element_type=jnp.float32)


def body(
    xbc,
    gate_z,
    dt_raw,
    dt_bias,
    a_log,
    skip_d,
    conv_weight,
    conv_bias,
    norm_gain,
    out_weight,
    starts,
):
    tok = xbc.shape[0]
    width = conv_weight.shape[0]
    chans = xbc.shape[1]
    groups = chans // GW
    heads = dt_raw.shape[0]
    rim, rim_flags = passed_along(
        (xbc[tok - (width - 1) :], starts[tok - (width - 1) :].astype(jnp.bfloat16)), "seq", 1
    )
    flags_int = rim_flags.astype(jnp.int32)
    after_rim = jnp.sum(flags_int) - jnp.cumsum(flags_int)
    counts = jnp.cumsum(starts)
    padded = jnp.concatenate([rim, xbc], axis=0).astype(jnp.float32)
    count_ext = jnp.concatenate([-after_rim, counts])
    acc = conv_bias[None, :] + conv_weight[width - 1][None, :] * xbc.astype(jnp.float32)
    for lag in range(1, width):
        shifted = padded[width - 1 - lag : width - 1 - lag + tok]
        keep = (count_ext[width - 1 - lag : width - 1 - lag + tok] == counts).astype(jnp.float32)
        acc = acc + conv_weight[width - 1 - lag][None, :] * shifted * keep[:, None]
    unit = jax.nn.silu(acc).astype(jnp.bfloat16)
    grid = unit.reshape(tok, groups, GW)
    xs = grid[:, :, : HG * P_SIZE].reshape(tok, heads, P_SIZE)
    bmat = grid[:, :, HG * P_SIZE : HG * P_SIZE + N]
    cmat = grid[:, :, HG * P_SIZE + N :]
    steps_dt = jax.nn.softplus(dt_raw.astype(jnp.float32) + dt_bias[:, None])
    logs = -jnp.exp(a_log)[:, None] * steps_dt
    length = min(128, tok)
    nblocks = tok // length
    x_blocks = xs.reshape(nblocks, length, heads, P_SIZE)
    b_blocks = bmat.reshape(nblocks, length, groups, N)
    c_blocks = cmat.reshape(nblocks, length, groups, N)
    dt_blocks = steps_dt.reshape(heads, nblocks, length).transpose(1, 0, 2)
    log_blocks = logs.reshape(heads, nblocks, length).transpose(1, 0, 2)
    start_blocks = starts.reshape(nblocks, length)
    items = (x_blocks, b_blocks, c_blocks, dt_blocks, log_blocks, start_blocks)

    def fold(carry, item):
        local, total = item
        return ((carry[0] * total, carry[1] * total[:, None, None] + local), None)

    y_diag, (locals_all, totals, enters) = lax.map(
        lambda item: (block_inner(item), block_local(item)), items
    )
    init = (jnp.ones((heads,), jnp.float32), jnp.zeros((heads, P_SIZE, N), jnp.float32))
    result, unused = lax.scan(fold, init, (locals_all, totals))
    entering = chain_states(result[0], result[1])

    def apply(state, item):
        cc, enter, local, total = item
        c_heads = jnp.repeat(cc, HG, axis=1)
        y_off = (
            jnp.einsum(
                "thn,hpn->thp",
                c_heads,
                state.astype(jnp.bfloat16),
                preferred_element_type=jnp.float32,
            )
            * enter.T[:, :, None]
        )
        return (state * total[:, None, None] + local, y_off)

    unused_state, y_offs = lax.scan(apply, entering, (c_blocks, enters, locals_all, totals))
    y_all = (y_diag + y_offs).reshape(tok, heads, P_SIZE) + skip_d[None, :, None] * xs.astype(
        jnp.float32
    )
    gated = y_all.reshape(tok, heads * P_SIZE) * jax.nn.silu(gate_z.astype(jnp.float32))
    total_sq = lax.psum(jnp.sum(gated * gated, axis=1), "head")
    normed = (gated * lax.rsqrt(total_sq / DI + 1e-05)[:, None] * norm_gain[None, :]).astype(
        jnp.bfloat16
    )
    terms = jnp.dot(
        normed,
        lax.all_gather(out_weight, "seq", axis=1, tiled=True),
        preferred_element_type=jnp.float32,
    )
    return lax.psum_scatter(terms.astype(jnp.bfloat16), "head", scatter_dimension=1, tiled=True)


def solution(mesh):
    placed = (
        P("seq", "head"),
        P("seq", "head"),
        P("head", "seq"),
        P("head"),
        P("head"),
        P("head"),
        P(None, "head"),
        P("head"),
        P("head"),
        P("head", "seq"),
        P("seq"),
    )
    return jax.shard_map(
        body, mesh=mesh, in_specs=placed, out_specs=P("seq", "head"), check_vma=False
    )
```

profile of v0, /device:TPU:2, one launch (start us, length us, event | category | flops | bytes accessed | tf_op | source)
XLA Modules:
  0.0 368.8 jit_solution(15041050396364430548)
XLA Ops:
  6.5 0.7 convert.4
  7.3 1.9 collective-permute-start.1
  9.2 0.7 slice.66
  10.0 3.5 collective-permute-start
  13.5 1.0 reduce-window.22
  14.8 0.9 slice_reduce_fusion.4
  15.7 0.7 exponential_negate_fusion
  16.4 0.8 compare_select_fusion
  17.5 0.7 convert_reduce_fusion
  18.2 0.7 negate_bitcast_fusion
  19.0 1.4 maximum_convert_fusion
  20.5 1.9 fusion.44
  22.4 0.9 copy-done.1
  23.3 1.9 reshape.277
  25.2 2.0 copy.38
  27.2 1.3 broadcast.139.clone
  28.5 17.6 %while.53 = (s32[]{:T(128)}, f32[3,128,16,64]{1,3,2,0:T(8,128)}, f32[3,16,64,128]{3,2,1,0:T(8,128)S(1)}, f32[3,16]{1,0:T(4,128)S(1)}, f32[3,16,128]{2,1,0:T(8,12...) while((s32[]{:T(128)}, f32[3,128,16,64]{1,3,2,0:T(8,128)}, ...), condition=%wide.region_7.8_spmd, body=%wide.region_4.7_spmd.sunk | while | flops 73752848 | bytes 2099011 | solution.py:129
  28.9 0.7 fusion.73
  29.8 0.6 slice.143
  31.4 0.7 compare_convert_fusion.2
  33.0 1.4 fusion.75
  34.7 0.7 fusion.73
  37.3 0.7 compare_convert_fusion.2
  38.9 1.4 fusion.75
  40.6 0.7 fusion.73
  43.2 0.7 compare_convert_fusion.2
  44.7 1.4 fusion.75
  46.7 0.8 copy-done
  47.5 0.7 all-gather.5.cloned.1.call-update
  48.4 1.3 dynamic-slice
  50.7 130.2 %all-reduce = f32[1024]{0:T(1024)S(1)} all-reduce(f32[1024]{0:T(1024)S(1)} %dynamic-update-slice), channel_id=2, replica_groups=mesh['seq'=64,'head'=8] {'seq'}, use_global_device_ids=true, to_apply=%add | all-reduce | flops 1024 | bytes 8192
  181.0 18.2 %all-gather.7.cloned.1.call-done = f32[1024,64,128]{2,1,0:T(8,128)} async-done(((f32[16,64,128]{2,1,0:T(8,128)}), f32[1024,64,128]{2,1,0:T(8,128)}) %all-gather.7.cloned.1.call-update) | async-done | bytes 33554448 | tf_op jit(solution)/shard_map/all_gather | solution.py:15
  199.3 2.5 while.54
  199.3 1.2 bitcast_add_fusion.6
  200.5 1.2 bitcast_add_fusion.6
  201.7 1.3 broadcast.139
  203.1 4.4 %while.55 = (s32[]{:T(128)}, f32[16,64,128]{2,1,0:T(8,128)S(1)}, f32[3,128,16,64]{1,3,2,0:T(8,128)}, f32[3,16]{1,0:T(4,128)S(1)}, f32[3,16,64,128]{3,2,1,0:T(8,1...) while((s32[]{:T(128)}, f32[16,64,128]{2,1,0:T(8,128)S(1)}, ...), condition=%wide.region_13.14_spmd, body=%wide.region_12.13_spmd.sunk | while | flops 34078720 | bytes 2745125 | solution.py:150
  203.1 1.3 fusion.81
  204.6 1.3 fusion.81
  206.0 1.3 fusion.81
  207.5 3.4 add.93
  210.9 2.3 copy.48
  213.2 1.8 reshape.278
  215.0 2.6 multiply_reduce_fusion.1
  217.6 17.0 %psum.7 = f32[384]{0:T(512)S(1)} all-reduce(f32[384]{0:T(512)S(1)} %get-tuple-element.329), channel_id=1, replica_groups=mesh['seq'=64,'head'=8] {'head'}, use_global_device_ids=true, to_apply=%region_15.16 | all-reduce | flops 384 | bytes 3072 | tf_op jit(solution)/shard_map/psum | solution.py:155
  234.6 53.6 %all-gather.5.cloned.1.call-done = bf16[1024,4096]{0,1:T(8,128)(2,1)} async-done(((bf16[1024,64]{0,1:T(8,128)(2,1)}), bf16[1024,4096]{0,1:T(8,128)(2,1)}) %all-gather.5.cloned.1.call-update) | async-done | bytes 8388624 | tf_op jit(solution)/shard_map/all_gather | solution.py:161
  288.3 10.2 %convolution_convert_fusion = bf16[384,4096]{1,0:T(8,128)(2,1)} fusion(bf16[1024,4096]{0,1:T(8,128)(2,1)} %all-gather.5.cloned.1.call-done, f32[384,1024]{1,0:T(8,128)S(1)} %get-tuple-element.330, f32[1024]{0:T(1024)S(1)} %copy-done.5, f32[384]{0:T(512)S(1)} %add_rsqrt_fusion), kind=kOutput, calls=%fused_computation.59 | convolution fusion | flops 3223977984 | bytes 13112832 | tf_op jit(solution)/shard_map/dot_general | solution.py:159
  298.5 63.8 %reduce-scatter.2.cloned.1.call-done = bf16[384,512]{1,0:T(8,128)(2,1)} async-done(((bf16[384,4096]{1,0:T(8,128)(2,1)}), bf16[384,512]{1,0:T(8,128)(2,1)}) %reduce-scatter.2.cloned.1.call-update) | async-done | bytes 393232 | tf_op jit(solution)/shard_map/reduce_scatter | solution.py:164
  (104 shorter events, 9.4 us)
Async XLA Ops:
  6.5 192.7 %all-gather.7.cloned.1.call-start = ((), (), s32[]{:S(2)}) async-start(), calls=%async_computation.3 | async-start | bytes 34078720 | tf_op jit(solution)/shard_map/all_gather | solution.py:15
  7.3 10.0 %collective-permute-start.1 = (bf16[3]{0:T(256)(128)(2,1)S(1)}, bf16[3]{0:T(256)(128)(2,1)S(1)}, u32[]{:S(2)}, u32[]{:S(2)}) collective-permute-start(bf16[3]{0:T(256)(128)(2,1)S(1)} %slice.68), channel_id=1, source_target_pairs={{0,8},{8,16},{16,24},{24,32},{32,40},{40,48},{48,56},{56,64},{64,7... | collective-permute-start | bytes 26 | tf_op jit(solution)/shard_map/ppermute | solution.py:29
  10.0 9.1 %collective-permute-start = (bf16[3,1280]{1,0:T(4,128)(2,1)S(1)}, bf16[3,1280]{1,0:T(4,128)(2,1)S(1)}, u32[]{:S(2)}, u32[]{:S(2)}) collective-permute-start(bf16[3,1280]{1,0:T(4,128)(2,1)S(1)} %slice.66), channel_id=1, source_target_pairs={{0,8},{8,16},{16,24},{24,32},{32,40},{40,48},{48,56},{56,64},{64,7... | collective-permute-start | bytes 23048 | tf_op jit(solution)/shard_map/ppermute | solution.py:29
  17.2 3.2 copy-start.2
  17.2 3.2 copy-start.3
  22.3 1.0 copy-start.1
  46.1 2.1 copy-start.4
  46.6 0.8 copy-start
  47.5 240.8 %all-gather.5.cloned.1.call-start = ((), (), s32[]{:S(2)}) async-start(), calls=%async_computation.1 | async-start | bytes 8519680 | tf_op jit(solution)/shard_map/all_gather | solution.py:161
  48.2 314.0 %reduce-scatter.2.cloned.1.call-start = ((), (), s32[]{:S(2)}) async-start(), calls=%async_computation.2 | async-start | bytes 3538944 | tf_op jit(solution)/shard_map/reduce_scatter | solution.py:164
  215.0 73.2 %copy-start.5 = (f32[1024]{0:T(1024)S(1)}, f32[1024]{0:T(1024)}, u32[]{:S(2)}) copy-start(f32[1024]{0:T(1024)} %param.27) | copy-start | bytes 12292
Sparse Core Ops, SparseCore 0:
  47.6 151.5 all-gather.6
  202.6 85.6 all-gather.4
  298.6 63.6 reduce-scatter.1
where the time goes:
time: 372 us; the launch traced here: 369 us
  blocking collectives  147 us (40%)
  waiting for transfers between devices  136 us (37%)
  other arithmetic  22.4 us (6%)
  local copies, waits for them, and re-layouts  20.7 us (6%)
  matrix products  20.1 us (5%)
  between operations  14 us (4%)
  starting transfers between devices  5.48 us (1%)
    unnamed x1, blocking collectives  130 us
    reduce_scatter x1, waiting for transfers between devices, body(): lax.psum_scatter(terms.astype(jnp.bfloat16), 'head', scatter_dimension=1,...  63.8 us
    all_gather x1, waiting for transfers between devices, body(): lax.all_gather(out_weight, 'seq', axis=1, tiled=True)  53.6 us
    all_gather x1, waiting for transfers between devices, carried_in(): gathered = jax.tree.map(lambda a: lax.all_gather(a, axis), part)  18.2 us
    psum x1, blocking collectives, body(): total_sq = lax.psum(jnp.sum(gated * gated, axis=1), 'head')  17 us
    dot_general x1, matrix products, body(): jnp.dot(normed, lax.all_gather(out_weight, 'seq', axis=1, tiled=True), pr...  10.2 us
  transfers between devices with their start and end apart: 5, of which 3 were waited for; matrix products, arithmetic and copies ran while one was open for 7% of the time, Pallas kernels for 0%

commit v1 on v0

--- a/solution.py
+++ b/solution.py
@@ -1,3 +1,4 @@
+import functools
 import jax
 import jax.numpy as jnp
 from jax import lax
@@ -8,6 +9,16 @@
 DI = 8192
 HG = 16
 GW = 1280
+
+
+def supply_ports(field_in, axis_tag):
+    state_next = lax.axis_size(axis_tag)
+    arr_now = jnp.stack(state_next * [field_in])
+    local_out = lax.all_to_all(arr_now, axis_tag, 0, 0)
+    return jnp.concatenate(local_out, axis=1)
+
+
+skins_lift = functools.partial(supply_ports, axis_tag="seq")
 
 
 def carried_in(part, axis, combine, identity):
@@ -156,11 +167,7 @@
     normed = (gated * lax.rsqrt(total_sq / DI + 1e-05)[:, None] * norm_gain[None, :]).astype(
         jnp.bfloat16
     )
-    terms = jnp.dot(
-        normed,
-        lax.all_gather(out_weight, "seq", axis=1, tiled=True),
-        preferred_element_type=jnp.float32,
-    )
+    terms = jnp.dot(normed, skins_lift(out_weight), preferred_element_type=jnp.float32)
     return lax.psum_scatter(terms.astype(jnp.bfloat16), "head", scatter_dimension=1, tiled=True)
 
 

time: 372 us -> 593 us (1.59)
  the two profiles are of different devices: /device:TPU:2 before, /device:TPU:6 now
where the time goes in v1:
time: 593 us; the launch traced here: 589 us
  blocking collectives  365 us (62%)
  waiting for transfers between devices  116 us (20%)
  other arithmetic  27.1 us (5%)
  local copies, waits for them, and re-layouts  24.9 us (4%)
  matrix products  20.1 us (3%)
  starting transfers between devices  19.3 us (3%)
  between operations  14.3 us (2%)
    unnamed x1, blocking collectives  347 us
    reduce_scatter x1, waiting for transfers between devices, body(): lax.psum_scatter(terms.astype(jnp.bfloat16), 'head', scatter_dimension=1,...  116 us
    psum x1, blocking collectives, body(): total_sq = lax.psum(jnp.sum(gated * gated, axis=1), 'head')  17.8 us
    all_to_all x1, starting transfers between devices, supply_ports(): local_out = lax.all_to_all(arr_now, axis_tag, 0, 0)  13 us
  transfers between devices with their start and end apart: 5, of which 1 were waited for; matrix products, arithmetic and copies ran while one was open for 6% of the time, Pallas kernels for 0%

profile of v1, /device:TPU:6, one launch (start us, length us, event | category | flops | bytes accessed | tf_op | source)
XLA Modules:
  0.0 589.3 jit_solution(7239803485912360249)
XLA Ops:
  7.3 1.9 collective-permute-start.1
  9.2 0.7 slice.66
  10.0 4.3 collective-permute-start
  14.3 1.0 reduce-window.22
  15.6 0.9 slice_reduce_fusion.4
  17.2 0.8 compare_select_fusion
  18.3 0.7 convert_reduce_fusion
  19.0 0.7 negate_bitcast_fusion
  19.8 1.4 maximum_convert_fusion
  21.3 1.9 fusion.44
  23.2 0.8 copy-done.1
  24.1 1.9 reshape.287
  26.0 2.0 copy.39
  28.0 1.3 broadcast.141.clone
  29.3 17.6 %while.53 = (s32[]{:T(128)}, f32[3,128,16,64]{1,3,2,0:T(8,128)}, f32[3,16,64,128]{3,2,1,0:T(8,128)S(1)}, f32[3,16]{1,0:T(4,128)S(1)}, f32[3,16,128]{2,1,0:T(8,12...) while((s32[]{:T(128)}, f32[3,128,16,64]{1,3,2,0:T(8,128)}, ...), condition=%wide.region_7.8_spmd, body=%wide.region_4.7_spmd.sunk | while | flops 73752848 | bytes 2099011 | solution.py:140
  29.6 0.7 fusion.73
  32.2 0.7 compare_convert_fusion.2
  33.8 1.4 fusion.75
  35.5 0.7 fusion.73
  38.1 0.7 compare_convert_fusion.2
  39.6 1.4 fusion.75
  41.4 0.7 fusion.73
  43.9 0.7 compare_convert_fusion.2
  45.5 1.4 fusion.75
  47.4 0.8 copy-done
  48.2 4.3 stack.2
  52.5 13.0 %all-to-all-start = ((bf16[64,1024,64]{1,2,0:T(8,128)(2,1)}), bf16[64,1024,64]{1,2,0:T(8,128)(2,1)}, u32[]{:S(2)}, u32[]{:S(2)}) async-start(bf16[64,1024,64]{1,2,0:T(8,128)(2,1)} %stack.2), calls=%async_computation | async-start | bytes 16777216 | tf_op jit(solution)/shard_map/all_to_all | solution.py:17
  65.8 1.3 dynamic-slice
  67.9 347.1 %all-reduce = f32[1024]{0:T(1024)S(1)} all-reduce(f32[1024]{0:T(1024)S(1)} %dynamic-update-slice), channel_id=2, replica_groups=mesh['seq'=64,'head'=8] {'seq'}, use_global_device_ids=true, to_apply=%add | all-reduce | flops 1024 | bytes 8192
  415.2 7.4 %while.54 = (s32[]{:T(128)}, f32[16,64,128]{2,1,0:T(8,128)S(1)}, s32[]{:T(128)}, f32[64,16]{1,0:T(8,128)S(1)}, f32[64,16,64,128]{3,2,1,0:T(8,128)}, /*index=5*/s32[]{:T(128)}, s32[]{:T(128)}, s32[]{:T(128)}) while((s32[]{:T(128)}, f32[16,64,128]{2,1,0:T(8,128)S(1)}, s32[]{:T(128)}, f32[64,16]{1,0:T(8,128)S(1)}, ...), condition=%wide.region_11.12_spmd, body=%wide.region_10.11_spmd.sunk | while | flops 262149 | bytes 1573183 | solution.py:34
  415.2 1.2 bitcast_add_fusion.6
  416.4 1.2 bitcast_add_fusion.6
  417.7 1.2 bitcast_add_fusion.6
  418.9 1.2 bitcast_add_fusion.6
  420.2 1.2 bitcast_add_fusion.6
  421.4 1.2 bitcast_add_fusion.6
  422.6 1.3 broadcast.141
  423.9 4.4 while.55
  423.9 1.3 fusion.81
  425.4 1.3 fusion.81
  426.9 1.3 fusion.81
  428.3 3.4 add.93
  431.7 2.3 copy.49
  434.0 1.8 reshape.288
  435.9 2.5 multiply_reduce_fusion.1
  438.4 17.8 %psum.7 = f32[384]{0:T(512)S(1)} all-reduce(f32[384]{0:T(512)S(1)} %get-tuple-element.329), channel_id=1, replica_groups=mesh['seq'=64,'head'=8] {'head'}, use_global_device_ids=true, to_apply=%region_15.16 | all-reduce | flops 384 | bytes 3072 | tf_op jit(solution)/shard_map/psum | solution.py:166
  456.2 10.2 %convolution_convert_fusion = bf16[384,4096]{1,0:T(8,128)(2,1)} fusion(bf16[1024,4096]{0,1:T(8,128)(2,1)} %bitcast.36, f32[384,1024]{1,0:T(8,128)S(1)} %get-tuple-element.330, f32[1024]{0:T(1024)S(1)} %copy-done.6, f32[384]{0:T(512)S(1)} %add_rsqrt_fusion), kind=kOutput, calls=%fused_computation.59 | convolution fusion | flops 3223977984 | bytes 13112832 | tf_op jit(solution)/shard_map/dot_general | solution.py:170
  466.4 116.0 %reduce-scatter.2.cloned.1.call-done = bf16[384,512]{1,0:T(8,128)(2,1)} async-done(((bf16[384,4096]{1,0:T(8,128)(2,1)}), bf16[384,512]{1,0:T(8,128)(2,1)}) %reduce-scatter.2.cloned.1.call-update) | async-done | bytes 393232 | tf_op jit(solution)/shard_map/reduce_scatter | solution.py:171
  (114 shorter events, 11.4 us)
Async XLA Ops:
  6.5 408.6 %all-gather.4.cloned.1.call-start = ((), (), s32[]{:S(2)}) async-start(), calls=%async_computation.3 | async-start | bytes 34078720 | tf_op jit(solution)/shard_map/all_gather | solution.py:26
  7.3 10.8 %collective-permute-start.1 = (bf16[3]{0:T(256)(128)(2,1)S(1)}, bf16[3]{0:T(256)(128)(2,1)S(1)}, u32[]{:S(2)}, u32[]{:S(2)}) collective-permute-start(bf16[3]{0:T(256)(128)(2,1)S(1)} %slice.68), channel_id=1, source_target_pairs={{0,8},{8,16},{16,24},{24,32},{32,40},{40,48},{48,56},{56,64},{64,7... | collective-permute-start | bytes 26 | tf_op jit(solution)/shard_map/ppermute | solution.py:40
  10.0 9.9 %collective-permute-start = (bf16[3,1280]{1,0:T(4,128)(2,1)S(1)}, bf16[3,1280]{1,0:T(4,128)(2,1)S(1)}, u32[]{:S(2)}, u32[]{:S(2)}) collective-permute-start(bf16[3,1280]{1,0:T(4,128)(2,1)S(1)} %slice.66), channel_id=1, source_target_pairs={{0,8},{8,16},{16,24},{24,32},{32,40},{40,48},{48,56},{56,64},{64,7... | collective-permute-start | bytes 23048 | tf_op jit(solution)/shard_map/ppermute | solution.py:40
  18.0 3.2 copy-start.2
  18.0 3.2 copy-start.4
  23.1 1.0 copy-start.1
  46.9 1.3 copy-start.3
  47.4 0.8 copy-start
  52.5 13.1 %copy-start.5 = (f32[16]{0:T(128)S(1)}, f32[16]{0:T(128)}, u32[]{:S(2)}) copy-start(f32[16]{0:T(128)} %param.24) | copy-start | bytes 196
  52.5 403.7 %all-to-all-start = ((bf16[64,1024,64]{1,2,0:T(8,128)(2,1)}), bf16[64,1024,64]{1,2,0:T(8,128)(2,1)}, u32[]{:S(2)}, u32[]{:S(2)}) async-start(bf16[64,1024,64]{1,2,0:T(8,128)(2,1)} %stack.2), calls=%async_computation | async-start | bytes 16777216 | tf_op jit(solution)/shard_map/all_to_all | solution.py:17
  65.5 516.9 %reduce-scatter.2.cloned.1.call-start = ((), (), s32[]{:S(2)}) async-start(), calls=%async_computation.2 | async-start | bytes 3538944 | tf_op jit(solution)/shard_map/reduce_scatter | solution.py:171
  435.9 20.3 %copy-start.6 = (f32[1024]{0:T(1024)S(1)}, f32[1024]{0:T(1024)}, u32[]{:S(2)}) copy-start(f32[1024]{0:T(1024)} %param.27) | copy-start | bytes 12292
Sparse Core Ops, SparseCore 0:
  48.3 302.0 all-gather.3
  466.5 115.8 reduce-scatter.1
